TPU v7x, 128 devices: a whole 4x4x4 slice. The times are simulated.
128 devices in a mesh: row: 8 (over y, z_lo), col: 16 (over z_hi, x, core).
Axes of the slice: x: 4, y: 4, z: 4 (z_hi: 2, z_lo: 2; z = z_hi * 2 + z_lo), core: 2. Of those that a mesh axis runs over, the one named last changes fastest.
Arguments:
- latents: bfloat16 [256, 256, 512], P('row', 'col'), may hold values from -6 to 6
- cotangent: bfloat16 [256, 256, 512], P('row', 'col'), may hold values from -6 to 6
- w_row: bfloat16 [4, 512, 512], replicated, may hold values from -6.6733202 to 6.6733202, as said below
- w_col: bfloat16 [4, 512, 512], replicated, may hold values from -6.6733202 to 6.6733202, as said below
- keep_heads: int32 [2, 8], replicated, may hold values 0 or 1
Outputs:
- output: bfloat16 [256, 256, 512], P('row', 'col')
- grad_latents: bfloat16 [256, 256, 512], P('row', 'col')
- grad_row: float32 [4, 512, 512], replicated
- grad_col: float32 [4, 512, 512], replicated
Inputs may be any that keep to these rules, and one draw needn't show every extreme that they name: `w_row`: projection weights. `w_col`: projection weights.
All inputs are finite; a program needn't handle non-finite values.
Results may differ from a plain program's by a relative error of at most 0.033.
Values may be sent and summed in bfloat16 or wider, within the bound.
No kernel may reach another device: no remote copies, remote signals or barrier semaphores. Data moves between devices by JAX's collectives and lax.ppermute only.
A program may use at most 128 MiB of HBM per device.

v0:
```python
import jax
import jax.numpy as jnp
from jax import lax
from jax.sharding import PartitionSpec as P

HEADS = 8
HEAD = 64


EPSILON = 1e-06


def mat_tn(left, right):
    return lax.dot_general(
        left, right, (((0,), (0,)), ((), ())), preferred_element_type=jnp.float32
    )


def mat_nt(left, right):
    return lax.dot_general(
        left, right, (((1,), (1,)), ((), ())), preferred_element_type=jnp.float32
    )


def head_specs(letters):
    if letters == "nl":
        return ("nlhe", "nmhe")
    return ("lnhe", "mnhe")


def line_forward(inputs, weights, head_gain, letters):
    in_shape = inputs.shape
    model_width = in_shape[2]
    q_spec, k_spec = head_specs(letters)
    values_f = inputs.astype(jnp.float32)
    inv_rms = lax.rsqrt(jnp.mean(values_f * values_f, axis=-1, keepdims=True) + EPSILON)
    normed = (values_f * inv_rms).astype(jnp.bfloat16).reshape(-1, model_width)

    def project(which_proj):
        result = jnp.dot(normed, weights[which_proj], preferred_element_type=jnp.float32)
        return result.astype(jnp.bfloat16).reshape(in_shape[0], in_shape[1], HEADS, HEAD)

    q_proj, k_proj, v_proj = (project(0), project(1), project(2))
    scores = jnp.einsum(
        q_spec + "," + k_spec + "->nhlm", q_proj, k_proj, preferred_element_type=jnp.float32
    ) * HEAD ** (-0.5)
    row_max = jnp.max(scores, axis=-1, keepdims=True)
    exp_scores = jnp.exp(scores - row_max)
    attn_probs = exp_scores / jnp.sum(exp_scores, axis=-1, keepdims=True)
    probs_low = attn_probs.astype(jnp.bfloat16)
    mixed_heads = jnp.einsum(
        "nhlm," + k_spec + "->" + q_spec, probs_low, v_proj, preferred_element_type=jnp.float32
    )
    attended = (mixed_heads * head_gain[:, None]).astype(jnp.bfloat16).reshape(-1, model_width)
    result = values_f + jnp.dot(attended, weights[3], preferred_element_type=jnp.float32).reshape(
        in_shape
    )
    saved_state = (normed, q_proj, k_proj, v_proj, attn_probs, probs_low, attended, inv_rms)
    return (result.astype(jnp.bfloat16), saved_state)


def line_backward(grad_out, inputs, saved_state, weights, head_gain, letters):
    normed, q_proj, k_proj, v_proj, attn_probs, probs_low, attended, inv_rms = saved_state
    in_shape = inputs.shape
    model_width = in_shape[2]
    q_spec, k_spec = head_specs(letters)
    grad_flat = grad_out.reshape(-1, model_width)
    grad_wo = mat_tn(attended, grad_flat)
    grad_att = mat_nt(grad_flat, weights[3]).reshape(in_shape[0], in_shape[1], HEADS, HEAD)
    grad_att = (grad_att * head_gain[:, None]).astype(jnp.bfloat16)
    grad_probs = jnp.einsum(
        q_spec + "," + k_spec + "->nhlm", grad_att, v_proj, preferred_element_type=jnp.float32
    )
    grad_scores = (
        attn_probs
        * (grad_probs - jnp.sum(attn_probs * grad_probs, axis=-1, keepdims=True))
        * HEAD ** (-0.5)
    )
    grad_scores = grad_scores.astype(jnp.bfloat16)
    grad_q = jnp.einsum(
        "nhlm," + k_spec + "->" + q_spec, grad_scores, k_proj, preferred_element_type=jnp.float32
    )
    grad_k = jnp.einsum(
        "nhlm," + q_spec + "->" + k_spec, grad_scores, q_proj, preferred_element_type=jnp.float32
    )
    grad_v = jnp.einsum(
        "nhlm," + q_spec + "->" + k_spec, probs_low, grad_att, preferred_element_type=jnp.float32
    )
    grad_q = grad_q.astype(jnp.bfloat16).reshape(-1, model_width)
    grad_k = grad_k.astype(jnp.bfloat16).reshape(-1, model_width)
    grad_v = grad_v.astype(jnp.bfloat16).reshape(-1, model_width)
    grad_weights = jnp.stack(
        [mat_tn(normed, grad_q), mat_tn(normed, grad_k), mat_tn(normed, grad_v), grad_wo]
    )
    grad_normed = (
        mat_nt(grad_q, weights[0]) + mat_nt(grad_k, weights[1]) + mat_nt(grad_v, weights[2])
    )
    values_f = inputs.astype(jnp.float32).reshape(-1, model_width)
    inv_flat = inv_rms.reshape(-1, 1)
    grad_in = grad_flat.astype(jnp.float32) + inv_flat * grad_normed
    grad_in = grad_in - values_f * inv_flat * inv_flat * inv_flat * jnp.mean(
        grad_normed * values_f, axis=-1, keepdims=True
    )
    return (grad_in.astype(jnp.bfloat16).reshape(in_shape), grad_weights)


def to_rows(values):
    return lax.all_to_all(values, "col", split_axis=0, concat_axis=1, tiled=True)


def from_rows(values):
    return lax.all_to_all(values, "col", split_axis=1, concat_axis=0, tiled=True)


def to_cols(values):
    return lax.all_to_all(values, "row", split_axis=1, concat_axis=0, tiled=True)


def from_cols(values):
    return lax.all_to_all(values, "row", split_axis=0, concat_axis=1, tiled=True)


def body(latents, cotangent, w_row, w_col, keep_heads):
    head_gain = keep_heads.astype(jnp.float32)
    rows_input = to_rows(latents)
    mid_rows, saved_row = line_forward(rows_input, w_row, head_gain[0], "nl")
    mid_cols = to_cols(from_rows(mid_rows))
    grad_cols = to_cols(cotangent)
    out_cols, saved_col = line_forward(mid_cols, w_col, head_gain[1], "ln")
    grad_mid_cols, grad_col = line_backward(
        grad_cols, mid_cols, saved_col, w_col, head_gain[1], "ln"
    )
    output = from_cols(out_cols)
    grad_mid_rows = to_rows(from_cols(grad_mid_cols))
    grad_in_rows, grad_row = line_backward(
        grad_mid_rows, rows_input, saved_row, w_row, head_gain[0], "nl"
    )
    grad_latents = from_rows(grad_in_rows)
    grad_row, grad_col = lax.psum((grad_row, grad_col), ("row", "col"))
    return (output, grad_latents, grad_row, grad_col)


def solution(mesh):
    in_specs = (P("row", "col", None), P("row", "col", None), P(), P(), P())
    out_specs = (P("row", "col", None), P("row", "col", None), P(), P())
    return jax.shard_map(body, mesh=mesh, in_specs=in_specs, out_specs=out_specs, check_vma=False)
```

profile of v0, /device:TPU:1, one launch (start us, length us, event | category | flops | bytes accessed | tf_op | source)
XLA Modules:
  0.0 423.8 jit_solution(3195072439449324358)
XLA Ops:
  7.2 9.1 %all-to-all-start = ((bf16[32,16,512]{2,1,0:T(8,128)(2,1)}), bf16[32,16,512]{2,1,0:T(8,128)(2,1)S(1)}, u32[]{:S(2)}, u32[]{:S(2)}) async-start(bf16[32,16,512]{2,1,0:T(8,128)(2,1)} %param.5), calls=%async_computation | async-start | bytes 1048576 | tf_op jit(solution)/shard_map/all_to_all | solution.py:108
  17.0 10.3 %all-to-all-done = bf16[32,16,512]{2,1,0:T(8,128)(2,1)S(1)} async-done(((bf16[32,16,512]{2,1,0:T(8,128)(2,1)}), bf16[32,16,512]{2,1,0:T(8,128)(2,1)S(1)}, u32[]{:S(2)}, u32[]{:S(2)}) %all-to-all-start) | async-done | bytes 524320 | tf_op jit(solution)/shard_map/all_to_all | solution.py:108
  27.8 1.8 convolution_convert_fusion.3
  32.6 1.8 reshape.285
  34.4 1.4 copy.243
  36.9 4.8 %fusion.124 = (f32[2,8,256]{2,1,0:T(8,128)S(1)}, f32[2,8,256,256]{2,3,1,0:T(8,128)}) fusion(bf16[2,256,8,64]{1,3,2,0:T(8,128)(2,1)} %copy.243, bf16[2,256,8,64]{1,3,2,0:T(8,128)(2,1)S(1)} %copy.244), kind=kOutput, calls=%fused_computation.143 | convolution fusion | flops 137363712 | bytes 5259264 | tf_op jit(solution)/shard_map/sub | solution.py:48
  41.7 2.8 fusion.46
  45.1 1.3 copy.248
  46.4 4.8 %all-to-all-start.1 = ((bf16[2,256,512]{2,0,1:T(2,128)(2,1)}), bf16[2,256,512]{2,0,1:T(2,128)(2,1)S(1)}, u32[]{:S(2)}, u32[]{:S(2)}) async-start(bf16[2,256,512]{2,0,1:T(2,128)(2,1)} %copy.248), calls=%async_computation.1 | async-start | bytes 1048576 | tf_op jit(solution)/shard_map/all_to_all | solution.py:112
  52.3 10.0 %all-to-all-done.1 = bf16[2,256,512]{2,0,1:T(2,128)(2,1)S(1)} async-done(((bf16[2,256,512]{2,0,1:T(2,128)(2,1)}), bf16[2,256,512]{2,0,1:T(2,128)(2,1)S(1)}, u32[]{:S(2)}, u32[]{:S(2)}) %all-to-all-start.1) | async-done | bytes 524320 | tf_op jit(solution)/shard_map/all_to_all | solution.py:112
  62.3 4.7 %all-to-all-start.4 = ((bf16[32,16,512]{2,0,1:T(8,128)(2,1)}), bf16[32,16,512]{2,0,1:T(8,128)(2,1)S(1)}, u32[]{:S(2)}, u32[]{:S(2)}) async-start(bf16[32,16,512]{2,0,1:T(8,128)(2,1)} %copy.263), calls=%async_computation.4 | async-start | bytes 1048576 | tf_op jit(solution)/shard_map/all_to_all | solution.py:116
  68.2 6.7 %all-to-all-done.4 = bf16[32,16,512]{2,0,1:T(8,128)(2,1)S(1)} async-done(((bf16[32,16,512]{2,0,1:T(8,128)(2,1)}), bf16[32,16,512]{2,0,1:T(8,128)(2,1)S(1)}, u32[]{:S(2)}, u32[]{:S(2)}) %all-to-all-start.4) | async-done | bytes 524320 | tf_op jit(solution)/shard_map/all_to_all | solution.py:116
  74.8 15.6 %all-to-all-start.2 = ((bf16[32,16,512]{2,0,1:T(8,128)(2,1)}), bf16[32,16,512]{2,0,1:T(8,128)(2,1)S(1)}, u32[]{:S(2)}, u32[]{:S(2)}) async-start(bf16[32,16,512]{2,0,1:T(8,128)(2,1)} %copy.251), calls=%async_computation.2 | async-start | bytes 1048576 | tf_op jit(solution)/shard_map/all_to_all | solution.py:116
  92.6 2.0 reshape.256
  94.6 2.4 fusion.50
  99.8 2.5 convolution_convert_fusion
  102.3 1.5 convolution_convert_fusion.1
  103.7 1.5 convolution_convert_fusion.2
  105.2 2.4 reshape.255
  107.6 2.8 copy.257
  110.4 1.5 reshape.254
  111.9 2.8 copy.256
  116.1 3.9 fusion.126
  120.1 3.5 fusion.125
  123.6 8.0 %fusion.57 = bf16[256,2,8,64]{0,3,2,1:T(8,128)(2,1)} fusion(bf16[256,2,8,64]{0,3,2,1:T(8,128)(2,1)S(1)} %copy-done.27, f32[2,8,256,256]{2,3,1,0:T(8,128)} %fusion.126, f32[2,8,256,256]{2,3,1,0:T(8,128)} %get-tuple-element.11, f32[2,8,256]{2,1,0:T(8,128)S(1)} %get-tuple-element.10), kind=kOutput, calls=%fused_computation.69 | convolution fusion | flops 141824256 | bytes 9453568 | tf_op jit(solution)/shard_map/nhlm,mnhe->lnhe/dot_general | solution.py:80
  131.6 8.1 %fusion.54 = bf16[256,2,8,64]{0,3,2,1:T(8,128)(2,1)} fusion(bf16[256,2,8,64]{0,3,2,1:T(8,128)(2,1)S(1)} %copy-done.28, f32[2,8,256,256]{2,3,1,0:T(8,128)} %fusion.126, f32[2,8,256,256]{2,3,1,0:T(8,128)} %get-tuple-element.11, f32[2,8,256]{2,1,0:T(8,128)S(1)} %get-tuple-element.10), kind=kOutput, calls=%fused_computation.68 | convolution fusion | flops 141824256 | bytes 9453568 | tf_op jit(solution)/shard_map/nhlm,lnhe->mnhe/dot_general | solution.py:83
  139.7 3.8 fusion.52
  143.8 1.8 copy.276
  145.6 1.9 reshape.270
  147.5 2.9 copy.275
  150.4 2.7 reshape.259
  153.2 2.9 copy.273
  156.1 2.5 reshape.258
  158.6 2.9 copy.270
  161.6 2.6 reshape.257
  164.1 1.8 fusion.81
  165.9 1.7 convolution_add_fusion.3
  169.5 2.0 reshape.260
  171.5 5.0 %all-to-all-start.5 = ((bf16[256,2,512]{2,1,0:T(2,128)(2,1)}), bf16[256,2,512]{2,1,0:T(2,128)(2,1)}, u32[]{:S(2)}, u32[]{:S(2)}) async-start(bf16[256,2,512]{2,1,0:T(2,128)(2,1)} %reshape.260), calls=%async_computation.5 | async-start | bytes 1048576 | tf_op jit(solution)/shard_map/all_to_all | solution.py:120
  176.5 2.9 fusion.47
  179.5 1.9 copy.294
  181.3 2.5 reshape.267
  183.9 2.6 convolution_bitcast_fusion.3
  186.4 2.5 convolution_bitcast_fusion.1
  191.2 6.1 %all-to-all-start.6 = ((bf16[32,16,512]{2,1,0:T(8,128)(2,1)}), bf16[32,16,512]{2,1,0:T(8,128)(2,1)}, u32[]{:S(2)}, u32[]{:S(2)}) async-start(bf16[32,16,512]{2,1,0:T(8,128)(2,1)} %copy.279), calls=%async_computation.6 | async-start | bytes 1048576 | tf_op jit(solution)/shard_map/all_to_all | solution.py:108
  198.2 1.8 convolution_bitcast_fusion
  200.0 2.4 pad_maximum_fusion.1
  202.4 5.9 %all-to-all-done.6 = bf16[32,16,512]{2,1,0:T(8,128)(2,1)} async-done(((bf16[32,16,512]{2,1,0:T(8,128)(2,1)}), bf16[32,16,512]{2,1,0:T(8,128)(2,1)}, u32[]{:S(2)}, u32[]{:S(2)}) %all-to-all-start.6) | async-done | bytes 524320 | tf_op jit(solution)/shard_map/all_to_all | solution.py:108
  209.9 3.8 fusion.53
  213.8 2.8 fusion.127
  216.5 8.1 %fusion.63 = bf16[2,256,8,64]{1,3,2,0:T(8,128)(2,1)} fusion(bf16[2,256,8,64]{1,3,2,0:T(8,128)(2,1)S(1)} %copy-done.25, f32[2,8,256,256]{2,3,1,0:T(8,128)} %fusion.127, f32[2,8,256,256]{2,3,1,0:T(8,128)} %get-tuple-element.9, f32[2,8,256]{2,1,0:T(8,128)S(1)} %get-tuple-element.8), kind=kOutput, calls=%fused_computation.71 | convolution fusion | flops 141824256 | bytes 9453568 | tf_op jit(solution)/shard_map/nhlm,nmhe->nlhe/dot_general | solution.py:80
  224.6 8.3 %fusion.60 = bf16[2,256,8,64]{1,3,2,0:T(8,128)(2,1)} fusion(bf16[2,256,8,64]{1,3,2,0:T(8,128)(2,1)} %copy.243, f32[2,8,256,256]{2,3,1,0:T(8,128)} %fusion.127, f32[2,8,256,256]{2,3,1,0:T(8,128)} %get-tuple-element.9, f32[2,8,256]{2,1,0:T(8,128)S(1)} %get-tuple-element.8), kind=kOutput, calls=%fused_computation.70 | convolution fusion | flops 141824256 | bytes 9453568 | tf_op jit(solution)/shard_map/nhlm,nlhe->nmhe/dot_general | solution.py:83
  232.9 1.7 copy.290
  238.8 2.5 pad_maximum_fusion
  241.5 1.7 fusion.49
  244.5 5.6 %all-to-all-start.3 = ((bf16[256,2,512]{2,1,0:T(2,128)(2,1)}), bf16[256,2,512]{2,1,0:T(2,128)(2,1)S(1)}, u32[]{:S(2)}, u32[]{:S(2)}) async-start(bf16[256,2,512]{2,1,0:T(2,128)(2,1)} %copy.261), calls=%async_computation.3 | async-start | bytes 1048576 | tf_op jit(solution)/shard_map/all_to_all | solution.py:120
  250.2 1.8 fusion.89
  252.0 1.5 convolution_add_fusion.1
  255.9 4.4 %all-to-all-done.3 = bf16[256,2,512]{2,1,0:T(2,128)(2,1)S(1)} async-done(((bf16[256,2,512]{2,1,0:T(2,128)(2,1)}), bf16[256,2,512]{2,1,0:T(2,128)(2,1)S(1)}, u32[]{:S(2)}, u32[]{:S(2)}) %all-to-all-start.3) | async-done | bytes 524320 | tf_op jit(solution)/shard_map/all_to_all | solution.py:120
  260.3 6.6 %all-to-all-start.7 = ((bf16[2,256,512]{2,0,1:T(2,128)(2,1)}), bf16[2,256,512]{2,0,1:T(2,128)(2,1)S(1)}, u32[]{:S(2)}, u32[]{:S(2)}) async-start(bf16[2,256,512]{2,0,1:T(2,128)(2,1)} %copy.291), calls=%async_computation.7 | async-start | bytes 1048576 | tf_op jit(solution)/shard_map/all_to_all | solution.py:112
  268.5 10.6 %all-to-all-done.7 = bf16[2,256,512]{2,0,1:T(2,128)(2,1)S(1)} async-done(((bf16[2,256,512]{2,0,1:T(2,128)(2,1)}), bf16[2,256,512]{2,0,1:T(2,128)(2,1)S(1)}, u32[]{:S(2)}, u32[]{:S(2)}) %all-to-all-start.7) | async-done | bytes 524320 | tf_op jit(solution)/shard_map/all_to_all | solution.py:112
  279.9 130.0 %all-reduce.3.cloned.1.call-done = (f32[4,512,512]{2,1,0:T(8,128)}, f32[4,512,512]{2,1,0:T(8,128)}) async-done(((f32[4,512,512]{2,1,0:T(8,128)}, f32[4,512,512]{2,1,0:T(8,128)}), (f32[4,512,512]{2,1,0:T(8,128)}, f32[4,512,512]{2,1,0:T(8,128)})) %all-reduce.3.cloned.1.call-update) | async-done | bytes 8388624 | tf_op jit(solution)/shard_map/psum | solution.py:139
  409.9 4.8 %copy.327 = f32[4,512,512]{2,1,0:T(8,128)} copy(f32[4,512,512]{2,1,0:T(8,128)} %get-tuple-element.18) | data formatting | bytes 8388608
  414.7 2.0 copy.328
  (133 shorter events, 31.3 us)
Async XLA Ops:
  7.2 20.1 %all-to-all-start = ((bf16[32,16,512]{2,1,0:T(8,128)(2,1)}), bf16[32,16,512]{2,1,0:T(8,128)(2,1)S(1)}, u32[]{:S(2)}, u32[]{:S(2)}) async-start(bf16[32,16,512]{2,1,0:T(8,128)(2,1)} %param.5), calls=%async_computation | async-start | bytes 1048576 | tf_op jit(solution)/shard_map/all_to_all | solution.py:108
  27.3 2.3 copy-start.16
  27.8 3.5 copy-start
  32.6 9.2 %copy-start.24 = (bf16[2,256,8,64]{1,3,2,0:T(8,128)(2,1)}, bf16[2,256,8,64]{1,3,2,0:T(8,128)(2,1)S(1)}, u32[]{:S(2)}) copy-start(bf16[2,256,8,64]{1,3,2,0:T(8,128)(2,1)S(1)} %copy.244) | copy-start | bytes 1572868
  36.9 7.6 %copy-start.19 = (bf16[2,256,8,64]{1,3,2,0:T(8,128)(2,1)}, bf16[2,256,8,64]{1,3,2,0:T(8,128)(2,1)S(1)}, u32[]{:S(2)}) copy-start(bf16[2,256,8,64]{1,3,2,0:T(8,128)(2,1)S(1)} %copy.245) | copy-start | bytes 1572868
  41.7 2.9 copy-start.17
  44.6 6.6 %copy-start.29 = (bf16[32,16,512]{2,1,0:T(8,128)(2,1)S(1)}, bf16[32,16,512]{2,1,0:T(8,128)(2,1)}, u32[]{:S(2)}) copy-start(bf16[32,16,512]{2,1,0:T(8,128)(2,1)} %param.6) | copy-start | bytes 1572868
  46.4 15.9 %all-to-all-start.1 = ((bf16[2,256,512]{2,0,1:T(2,128)(2,1)}), bf16[2,256,512]{2,0,1:T(2,128)(2,1)S(1)}, u32[]{:S(2)}, u32[]{:S(2)}) async-start(bf16[2,256,512]{2,0,1:T(2,128)(2,1)} %copy.248), calls=%async_computation.1 | async-start | bytes 1048576 | tf_op jit(solution)/shard_map/all_to_all | solution.py:112
  62.3 12.5 %all-to-all-start.4 = ((bf16[32,16,512]{2,0,1:T(8,128)(2,1)}), bf16[32,16,512]{2,0,1:T(8,128)(2,1)S(1)}, u32[]{:S(2)}, u32[]{:S(2)}) async-start(bf16[32,16,512]{2,0,1:T(8,128)(2,1)} %copy.263), calls=%async_computation.4 | async-start | bytes 1048576 | tf_op jit(solution)/shard_map/all_to_all | solution.py:116
  67.0 27.6 %slice-start = ((bf16[4,512,512]{2,1,0:T(8,128)(2,1)}), bf16[1,512,512]{2,1,0:T(8,128)(2,1)S(1)}, s32[]{:S(2)}) async-start(bf16[4,512,512]{2,1,0:T(8,128)(2,1)} %param.8), calls=%async_computation.9 | async-start | bytes 1048576 | tf_op jit(solution)/shard_map/slice | solution.py:55
  74.8 23.7 %all-to-all-start.2 = ((bf16[32,16,512]{2,0,1:T(8,128)(2,1)}), bf16[32,16,512]{2,0,1:T(8,128)(2,1)S(1)}, u32[]{:S(2)}, u32[]{:S(2)}) async-start(bf16[32,16,512]{2,0,1:T(8,128)(2,1)} %copy.251), calls=%async_computation.2 | async-start | bytes 1048576 | tf_op jit(solution)/shard_map/all_to_all | solution.py:116
  99.8 12.2 %copy-start.2 = (bf16[512,512]{1,0:T(8,128)(2,1)}, bf16[512,512]{1,0:T(8,128)(2,1)S(1)}, u32[]{:S(2)}) copy-start(bf16[512,512]{1,0:T(8,128)(2,1)S(1)} %convert_element_type.216) | copy-start | bytes 1572868
  116.1 7.5 %copy-start.22 = (bf16[256,2,8,64]{0,3,2,1:T(8,128)(2,1)}, bf16[256,2,8,64]{0,3,2,1:T(8,128)(2,1)S(1)}, u32[]{:S(2)}) copy-start(bf16[256,2,8,64]{0,3,2,1:T(8,128)(2,1)S(1)} %copy.258) | copy-start | bytes 1572868
  116.1 4.0 copy-start.27
  116.1 4.0 copy-start.28
  131.6 8.1 %copy-start.26 = (bf16[256,2,8,64]{0,3,2,1:T(8,128)(2,1)S(1)}, bf16[256,2,8,64]{0,3,2,1:T(8,128)(2,1)}, u32[]{:S(2)}) copy-start(bf16[256,2,8,64]{0,3,2,1:T(8,128)(2,1)} %fusion.50) | copy-start | bytes 1572868
  164.1 3.6 copy-start.9
  164.1 3.6 copy-start.15
  165.9 2.3 copy-start.5
  171.5 17.4 %all-to-all-start.5 = ((bf16[256,2,512]{2,1,0:T(2,128)(2,1)}), bf16[256,2,512]{2,1,0:T(2,128)(2,1)}, u32[]{:S(2)}, u32[]{:S(2)}) async-start(bf16[256,2,512]{2,1,0:T(2,128)(2,1)} %reshape.260), calls=%async_computation.5 | async-start | bytes 1048576 | tf_op jit(solution)/shard_map/all_to_all | solution.py:120
  176.5 7.3 %copy-start.3 = (bf16[512,512]{1,0:T(8,128)(2,1)S(1)}, bf16[512,512]{1,0:T(8,128)(2,1)}, u32[]{:S(2)}) copy-start(bf16[512,512]{1,0:T(8,128)(2,1)} %copy-done.2) | copy-start | bytes 1572868
  179.5 1.9 copy-start.21
  183.9 13.8 %copy-start.4 = (bf16[512,512]{1,0:T(8,128)(2,1)S(1)}, bf16[512,512]{1,0:T(8,128)(2,1)}, u32[]{:S(2)}) copy-start(bf16[512,512]{1,0:T(8,128)(2,1)} %reshape.258) | copy-start | bytes 1572868
  191.2 17.2 %all-to-all-start.6 = ((bf16[32,16,512]{2,1,0:T(8,128)(2,1)}), bf16[32,16,512]{2,1,0:T(8,128)(2,1)}, u32[]{:S(2)}, u32[]{:S(2)}) async-start(bf16[32,16,512]{2,1,0:T(8,128)(2,1)} %copy.279), calls=%async_computation.6 | async-start | bytes 1048576 | tf_op jit(solution)/shard_map/all_to_all | solution.py:108
  197.2 212.6 %all-reduce.3.cloned.1.call-start = ((), (), s32[]{:S(2)}) async-start(), calls=%async_computation.8 | async-start | bytes 16777216 | tf_op jit(solution)/shard_map/psum | solution.py:139
  197.7 2.3 copy-start.13
  197.7 2.3 copy-start.14
  200.0 9.4 %slice-start.1 = ((bf16[4,512,512]{2,1,0:T(8,128)(2,1)}), bf16[1,512,512]{2,1,0:T(8,128)(2,1)S(1)}, s32[]{:S(2)}) async-start(bf16[4,512,512]{2,1,0:T(8,128)(2,1)} %param.7), calls=%async_computation.10 | async-start | bytes 1048576 | tf_op jit(solution)/shard_map/slice | solution.py:55
  209.9 3.8 copy-start.20
  213.8 2.8 copy-start.25
  224.6 10.9 %copy-start.1 = (bf16[2,16,16,512]{3,2,1,0:T(8,128)(2,1)S(1)}, bf16[2,16,16,512]{3,2,1,0:T(8,128)(2,1)}, u32[]{:S(2)}) copy-start(bf16[2,16,16,512]{3,2,1,0:T(8,128)(2,1)} %copy-done) | copy-start | bytes 1572868
  232.9 3.1 copy-start.31
  232.9 3.8 copy-start.30
  234.7 0.9 copy-start.10
  236.0 2.3 copy-start.23
  236.7 1.6 copy-start.6
  237.4 1.0 copy-start.8
  241.4 10.6 %copy-start.7 = (bf16[64,8,2,256]{3,1,2,0:T(8,128)(2,1)S(1)}, bf16[64,8,2,256]{3,1,2,0:T(8,128)(2,1)}, u32[]{:S(2)}) copy-start(bf16[64,8,2,256]{3,1,2,0:T(8,128)(2,1)} %copy-done.6) | copy-start | bytes 1572868
  243.2 10.4 %copy-start.11 = (bf16[64,8,2,256]{3,1,2,0:T(8,128)(2,1)S(1)}, bf16[64,8,2,256]{3,1,2,0:T(8,128)(2,1)}, u32[]{:S(2)}) copy-start(bf16[64,8,2,256]{3,1,2,0:T(8,128)(2,1)} %copy-done.10) | copy-start | bytes 1572868
  244.5 15.8 %all-to-all-start.3 = ((bf16[256,2,512]{2,1,0:T(2,128)(2,1)}), bf16[256,2,512]{2,1,0:T(2,128)(2,1)S(1)}, u32[]{:S(2)}, u32[]{:S(2)}) async-start(bf16[256,2,512]{2,1,0:T(2,128)(2,1)} %copy.261), calls=%async_computation.3 | async-start | bytes 1048576 | tf_op jit(solution)/shard_map/all_to_all | solution.py:120
  250.2 3.4 copy-start.18
  260.3 18.7 %all-to-all-start.7 = ((bf16[2,256,512]{2,0,1:T(2,128)(2,1)}), bf16[2,256,512]{2,0,1:T(2,128)(2,1)S(1)}, u32[]{:S(2)}, u32[]{:S(2)}) async-start(bf16[2,256,512]{2,0,1:T(2,128)(2,1)} %copy.291), calls=%async_computation.7 | async-start | bytes 1048576 | tf_op jit(solution)/shard_map/all_to_all | solution.py:112
  409.9 4.8 %copy-start.12 = (f32[4,512,512]{2,1,0:T(8,128)S(1)}, f32[4,512,512]{2,1,0:T(8,128)}, u32[]{:S(2)}) copy-start(f32[4,512,512]{2,1,0:T(8,128)} %get-tuple-element.19) | copy-start | bytes 12582916
Sparse Core Ops, SparseCore 0:
  241.4 168.4 all-reduce.2
where the time goes:
time: 432 us; the launch traced here: 424 us
  waiting for transfers between devices  178 us (41%)
  matrix products  92 us (21%)
  local copies, waits for them, and re-layouts  72.8 us (17%)
  starting transfers between devices  58 us (13%)
  between operations  14.9 us (3%)
  other arithmetic  8.02 us (2%)
    psum x1, waiting for transfers between devices, body(): grad_row, grad_col = lax.psum((grad_row, grad_col), ('row', 'col'))  130 us
    all_to_all x2, waiting for transfers between devices, from_rows(): lax.all_to_all(values, 'col', split_axis=1, concat_axis=0, tiled=True)  20.6 us
    all_to_all x2, starting transfers between devices, to_cols(): lax.all_to_all(values, 'row', split_axis=1, concat_axis=0, tiled=True)  20.3 us
    dot_general x2, matrix products, line_backward(): jnp.einsum('nhlm,' + q_spec + '->' + k_spec, grad_scores, q_proj, preferr...  16.4 us
    reshape x12, local copies, waits for them, and re-layouts, project(): result.astype(jnp.bfloat16).reshape(in_shape[0], in_shape[1], HEADS, HEAD)  16.3 us
    all_to_all x2, waiting for transfers between devices, to_rows(): lax.all_to_all(values, 'col', split_axis=0, concat_axis=1, tiled=True)  16.2 us
    dot_general x2, matrix products, line_backward(): jnp.einsum('nhlm,' + k_spec + '->' + q_spec, grad_scores, k_proj, preferr...  16.1 us
    all_to_all x2, starting transfers between devices, to_rows(): lax.all_to_all(values, 'col', split_axis=0, concat_axis=1, tiled=True)  15.2 us
  transfers between devices with their start and end apart: 9, of which 8 were waited for; matrix products, arithmetic and copies ran while one was open for 9% of the time, Pallas kernels for 0%

commit v1 on v0

v1 whole, which is shorter than its diff:
```python
import functools

import jax
import jax.numpy as jnp
from jax import lax
from jax.experimental import pallas as pl
from jax.experimental.pallas import tpu as pltpu
from jax.sharding import Mesh, PartitionSpec as P

HEADS = 8
HEAD = 64
D = 512
PAIR = 128
N_PAIR = D // PAIR
LINE = 256
TOK = 512
N_ROW = 8
N_COL = 16
N_DEV = N_ROW * N_COL
EPSILON = 1e-06
SCALE = HEAD ** (-0.5)

F32 = jnp.float32
BF16 = jnp.bfloat16

ROW = ("y", "zl")
COL = ("zh", "x", "c")
BOTH = COL + ROW
CHIPS = ("y", "zl", "zh", "x")


def dot(left, right):
    return lax.dot_general(left, right, (((1,), (0,)), ((), ())), preferred_element_type=F32)


def dot_nt(left, right):
    return lax.dot_general(left, right, (((1,), (1,)), ((), ())), preferred_element_type=F32)


def dot_tn(left, right):
    return lax.dot_general(left, right, (((0,), (0,)), ((), ())), preferred_element_type=F32)


def halves(value):
    lane = lax.broadcasted_iota(jnp.int32, value.shape, 1)
    zero = jnp.zeros_like(value)
    return (jnp.where(lane < HEAD, value, zero), jnp.where(lane >= HEAD, value, zero))


def inverse_rms(values_f):
    return lax.rsqrt(jnp.mean(values_f * values_f, axis=-1, keepdims=True) + EPSILON)


def softmax(q_half, k_pair):
    scores = dot_nt(q_half, k_pair)
    peak = jnp.max(scores, axis=-1, keepdims=True)
    grown = jnp.exp(scores - peak)
    return grown * (1.0 / jnp.sum(grown, axis=-1, keepdims=True))


def slot(col_local, group, row_local):
    return col_local * 8 + group * 2 + row_local


def row_forward_kernel(x_ref, w_ref, gain_ref, mid_ref, qkv_ref, att_ref, n_s, mix_s):
    for rr in range(2):
        u = x_ref[:, rr].astype(F32).reshape(LINE, D)
        n_s[rr * LINE : (rr + 1) * LINE, :] = (u * inverse_rms(u)).astype(BF16)
    normed = n_s[...]
    qkv_ref[0] = (dot(normed, w_ref[0]).astype(BF16).astype(F32) * SCALE).astype(BF16)
    qkv_ref[1] = dot(normed, w_ref[1]).astype(BF16)
    qkv_ref[2] = dot(normed, w_ref[2]).astype(BF16)
    for rr in range(2):
        rows = slice(rr * LINE, (rr + 1) * LINE)
        for pair in range(N_PAIR):
            lanes = slice(pair * PAIR, (pair + 1) * PAIR)
            q_half = halves(qkv_ref[0, rows, lanes])
            v_half = halves(qkv_ref[2, rows, lanes])
            k_pair = qkv_ref[1, rows, lanes]
            probs = [softmax(q_half[h], k_pair).astype(BF16) for h in range(2)]
            mixed = dot(probs[0], v_half[0]) + dot(probs[1], v_half[1])
            att_ref[rows, lanes] = (mixed * gain_ref[:, lanes]).astype(BF16)
    added = dot(att_ref[...], w_ref[3])
    for rr in range(2):
        u = x_ref[:, rr].astype(F32).reshape(LINE, D)
        mid = (u + added[rr * LINE : (rr + 1) * LINE]).reshape(16, 2, 8, D)
        for cc in range(2):
            for group in range(4):
                piece = mid[:, cc, :, group * 128 : (group + 1) * 128].reshape(128, 128)
                mix_s[pl.ds(slot(cc, group, rr), 128, stride=16), :] = piece
    mid_ref[...] = mix_s[...].reshape(N_DEV, 16, 128).astype(BF16)


def attention_backward(rows, lanes, qkv, da_ref, probs_of, dqkv_ref):
    q_half = halves(qkv[0, rows, lanes])
    k_pair = qkv[1, rows, lanes]
    k_half = halves(k_pair)
    v_pair = qkv[2, rows, lanes]
    da_half = halves(da_ref[rows, lanes])
    grads = []
    lows = []
    for h in range(2):
        probs = probs_of(h, q_half, k_pair)
        lows.append(probs.astype(BF16))
        grad_probs = dot_nt(da_half[h], v_pair)
        total = jnp.sum(probs * grad_probs, axis=-1, keepdims=True)
        grads.append((probs * (grad_probs - total)).astype(BF16))
    dqkv_ref[0, rows, lanes] = (
        (dot(grads[0], k_half[0]) + dot(grads[1], k_half[1])) * SCALE
    ).astype(BF16)
    dqkv_ref[1, rows, lanes] = (
        dot_tn(grads[0], q_half[0]) + dot_tn(grads[1], q_half[1])
    ).astype(BF16)
    dqkv_ref[2, rows, lanes] = (
        dot_tn(lows[0], da_half[0]) + dot_tn(lows[1], da_half[1])
    ).astype(BF16)
    return lows


def input_gradient(grad_f, u, dqkv_ref, w_ref, rows):
    inv = inverse_rms(u)
    dn = (
        dot_nt(dqkv_ref[0, rows, :], w_ref[0])
        + dot_nt(dqkv_ref[1, rows, :], w_ref[1])
        + dot_nt(dqkv_ref[2, rows, :], w_ref[2])
    )
    mean = jnp.mean(dn * u, axis=-1, keepdims=True)
    return grad_f + inv * dn - u * (inv * inv * inv * mean)


def recomputed(h, q_half, k_pair):
    return softmax(q_half[h], k_pair)


def row_backward_kernel(
    g_ref, x_ref, qkv_ref, att_ref, w_ref, gain_ref, gin_ref, dw_ref, mix_s, g_s, da_s, dqkv_s, n_s
):
    mix_s[...] = g_ref[...].astype(F32).reshape(N_DEV * 16, 128)
    for rr in range(2):
        for cc in range(2):
            for group in range(4):
                piece = mix_s[pl.ds(slot(cc, group, rr), 128, stride=16), :]
                g_s[rr, :, cc, :, group * 128 : (group + 1) * 128] = piece.reshape(16, 8, 128)
    grad_f = g_s[...].reshape(TOK, D)
    grad_low = grad_f.astype(BF16)
    da_s[...] = (dot_nt(grad_low, w_ref[3]) * gain_ref[...]).astype(BF16)
    for rr in range(2):
        u = x_ref[:, rr].astype(F32).reshape(LINE, D)
        n_s[rr * LINE : (rr + 1) * LINE, :] = (u * inverse_rms(u)).astype(BF16)
        rows = slice(rr * LINE, (rr + 1) * LINE)
        for pair in range(N_PAIR):
            lanes = slice(pair * PAIR, (pair + 1) * PAIR)
            attention_backward(rows, lanes, qkv_ref, da_s, recomputed, dqkv_s)
    for which in range(3):
        dw_ref[which] = dot_tn(n_s[...], dqkv_s[which]).astype(BF16)
    dw_ref[3] = dot_tn(att_ref[...], grad_low).astype(BF16)
    for rr in range(2):
        rows = slice(rr * LINE, (rr + 1) * LINE)
        u = x_ref[:, rr].astype(F32).reshape(LINE, D)
        grad_in = input_gradient(g_s[rr].reshape(LINE, D), u, dqkv_s, w_ref, rows)
        gin_ref[:, rr] = grad_in.astype(BF16).reshape(16, 16, D)


def col_kernel(
    m_ref, c_ref, w_ref, gain_ref, out_ref, gmid_ref, dw_ref,
    mix_s, u_s, g_s, n_s, qkv_s, att_s, da_s, dqkv_s, p_s,
):
    mix_s[...] = m_ref[...].astype(F32).reshape(N_DEV * 16, 128)
    for cc in range(2):
        for rr in range(2):
            base = cc * LINE + rr * 128
            g_s[base : base + 128, :] = c_ref[:, cc, rr * 16 : (rr + 1) * 16, :].reshape(128, D)
            for group in range(4):
                for grid_row in range(N_ROW):
                    start = base + grid_row * 16
                    u_s[start : start + 16, group * 128 : (group + 1) * 128] = mix_s[
                        pl.ds(grid_row * 16 + slot(cc, group, rr), 16, stride=128), :
                    ]
    da_s[...] = (dot_nt(g_s[...], w_ref[3]) * gain_ref[...]).astype(BF16)
    u = u_s[...]
    n_s[...] = (u * inverse_rms(u)).astype(BF16)
    normed = n_s[...]
    qkv_s[0] = (dot(normed, w_ref[0]).astype(BF16).astype(F32) * SCALE).astype(BF16)
    qkv_s[1] = dot(normed, w_ref[1]).astype(BF16)
    qkv_s[2] = dot(normed, w_ref[2]).astype(BF16)
    for cc in range(2):
        rows = slice(cc * LINE, (cc + 1) * LINE)
        for pair in range(N_PAIR):
            lanes = slice(pair * PAIR, (pair + 1) * PAIR)
            lows = attention_backward(rows, lanes, qkv_s, da_s, recomputed, dqkv_s)
            v_half = halves(qkv_s[2, rows, lanes])
            mixed = dot(lows[0], v_half[0]) + dot(lows[1], v_half[1])
            att_s[rows, lanes] = (mixed * gain_ref[:, lanes]).astype(BF16)
    for cc in range(2):
        rows = slice(cc * LINE, (cc + 1) * LINE)
        u = u_s[rows, :]
        grad_in = input_gradient(g_s[rows, :].astype(F32), u, dqkv_s, w_ref, rows)
        for rr in range(2):
            for group in range(4):
                for grid_row in range(N_ROW):
                    start = rr * 128 + grid_row * 16
                    mix_s[pl.ds(grid_row * 16 + slot(cc, group, rr), 16, stride=128), :] = grad_in[
                        start : start + 16, group * 128 : (group + 1) * 128
                    ]
    gmid_ref[...] = mix_s[...].reshape(N_DEV, 16, 128).astype(BF16)
    for cc in range(2):
        rows = slice(cc * LINE, (cc + 1) * LINE)
        result = (u_s[rows, :] + dot(att_s[rows, :], w_ref[3])).astype(BF16)
        for rr in range(2):
            out_ref[:, cc, rr * 16 : (rr + 1) * 16, :] = result[rr * 128 : (rr + 1) * 128].reshape(
                8, 16, D
            )
    for which in range(3):
        dw_ref[which] = dot_tn(n_s[...], dqkv_s[which]).astype(BF16)
    dw_ref[3] = dot_tn(att_s[...], g_s[...]).astype(BF16)


def tile_to_lines_kernel(tile_ref, lines_ref, mix_s):
    tile = tile_ref[...].astype(F32).reshape(TOK, D)
    for group in range(4):
        lanes = slice(group * 128, (group + 1) * 128)
        mix_s[group] = tile[:, lanes]
        for grid_row in range(N_ROW):
            for cc in range(2):
                for rr in range(2):
                    piece = mix_s[group, pl.ds(rr * 16 + cc * 8 + grid_row, 16, stride=32), :]
                    lines_ref[grid_row, cc, rr * 16 : (rr + 1) * 16, lanes] = piece.astype(BF16)


def lines_to_tile_kernel(lines_ref, tile_ref, mix_s):
    for group in range(4):
        lanes = slice(group * 128, (group + 1) * 128)
        for grid_row in range(N_ROW):
            for cc in range(2):
                for rr in range(2):
                    piece = lines_ref[grid_row, cc, rr * 16 : (rr + 1) * 16, lanes].astype(F32)
                    mix_s[group, pl.ds(rr * 16 + cc * 8 + grid_row, 16, stride=32), :] = piece
        tile_ref[:, :, lanes] = mix_s[group].astype(BF16).reshape(32, 16, 128)


def call(kernel, outs, scratch, flops, moved, name):
    return pl.pallas_call(
        kernel,
        out_shape=outs,
        scratch_shapes=scratch,
        name=name,
        compiler_params=pltpu.CompilerParams(vmem_limit_bytes=40 * 1024 * 1024),
        cost_estimate=pl.CostEstimate(flops=flops, bytes_accessed=moved, transcendentals=0),
    )


def shape(*dims, dtype=BF16):
    return jax.ShapeDtypeStruct(dims, dtype)


MATMUL = 2 * TOK * D * D
ATTEND = 2 * 16 * LINE * LINE * HEAD
MIB = 1 << 20

row_forward = call(
    row_forward_kernel,
    (shape(N_DEV, 16, 128), shape(3, TOK, D), shape(TOK, D)),
    [pltpu.VMEM((TOK, D), BF16), pltpu.VMEM((N_DEV * 16, 128), F32)],
    4 * MATMUL + 2 * ATTEND,
    6 * MIB,
    "row_forward",
)
row_backward = call(
    row_backward_kernel,
    (shape(16, 2, 16, D), shape(4, D, D)),
    [
        pltpu.VMEM((N_DEV * 16, 128), F32),
        pltpu.VMEM((2, 16, 2, 8, D), F32),
        pltpu.VMEM((TOK, D), BF16),
        pltpu.VMEM((3, TOK, D), BF16),
        pltpu.VMEM((TOK, D), BF16),
    ],
    8 * MATMUL + 5 * ATTEND,
    8 * MIB,
    "row_backward",
)
col_both = call(
    col_kernel,
    (shape(8, 2, 32, D), shape(N_DEV, 16, 128), shape(4, D, D)),
    [
        pltpu.VMEM((N_DEV * 16, 128), F32),
        pltpu.VMEM((TOK, D), F32),
        pltpu.VMEM((TOK, D), BF16),
        pltpu.VMEM((TOK, D), BF16),
        pltpu.VMEM((3, TOK, D), BF16),
        pltpu.VMEM((TOK, D), BF16),
        pltpu.VMEM((TOK, D), BF16),
        pltpu.VMEM((3, TOK, D), BF16),
        pltpu.VMEM((8, 128), F32),
    ],
    12 * MATMUL + 6 * ATTEND,
    6 * MIB,
    "col_both",
)
tile_to_lines = call(
    tile_to_lines_kernel, shape(8, 2, 32, D), [pltpu.VMEM((4, TOK, 128), F32)], 0, MIB, "tile_to_lines"
)
lines_to_tile = call(
    lines_to_tile_kernel, shape(32, 16, D), [pltpu.VMEM((4, TOK, 128), F32)], 0, MIB, "lines_to_tile"
)


def exchange(values, axes):
    return lax.all_to_all(values, axes, split_axis=0, concat_axis=0, tiled=True)


def reduce_all(partial):
    pieces = partial.reshape(2, 1024, 512)
    both = exchange(pieces, ("c",))
    mine = (both[0].astype(F32) + both[1].astype(F32)).astype(BF16)
    parts = exchange(mine.reshape(64, 64, 128), CHIPS)
    total = jnp.sum(parts.astype(F32), axis=0).astype(BF16)
    spread = exchange(jnp.broadcast_to(total[None], (64, 64, 128)), CHIPS)
    whole = exchange(jnp.broadcast_to(spread.reshape(1, 1024, 512), (2, 1024, 512)), ("c",))
    return whole.reshape(4, D, D).astype(F32)


def body(latents, cotangent, w_row, w_col, keep_heads):
    gain = jnp.repeat(keep_heads.astype(F32), HEAD, axis=1)
    gain_row, gain_col = gain[0:1], gain[1:2]
    rows_in = exchange(latents.reshape(16, 2, 16, D), COL)
    grad_lines = exchange(tile_to_lines(cotangent), ROW)
    mid_send, qkv_row, att_row = row_forward(rows_in, w_row, gain_row)
    mid_lines = exchange(mid_send, BOTH)
    out_lines, grad_send, part_col = col_both(mid_lines, grad_lines, w_col, gain_col)
    grad_rows = exchange(grad_send, BOTH)
    output = lines_to_tile(exchange(out_lines, ROW))
    grad_in, part_row = row_backward(grad_rows, rows_in, qkv_row, att_row, w_row, gain_row)
    grad_latents = exchange(grad_in, COL).reshape(32, 16, D)
    return (output, grad_latents, reduce_all(part_row), reduce_all(part_col))


def solution(mesh):
    fine = Mesh(mesh.devices.reshape(4, 2, 2, 4, 2), ("y", "zl", "zh", "x", "c"))
    tile = P(ROW, COL, None)
    return jax.shard_map(
        body,
        mesh=fine,
        in_specs=(tile, tile, P(), P(), P()),
        out_specs=(tile, tile, P(), P()),
        check_vma=False,
    )
```

time: 432 us -> 250 us (0.58); the launches traced: 424 us -> 248 us
  waiting for transfers between devices: 178 us -> 74.8 us
  matrix products: 92 us -> 0 us
  blocking collectives: 0 us -> 64 us
  local copies, waits for them, and re-layouts: 72.8 us -> 19.8 us
  Pallas kernels: 0 us -> 29.5 us
  between operations: 14.9 us -> 0.78 us
  starting transfers between devices: 58 us -> 50 us
    psum x1 -> x0, waiting for transfers between devices: 130 us -> none  [body(): grad_row, grad_col = lax.psum((grad_row, grad_col), ('row', 'col'))]
    dot_general x34 -> x0, matrix products: 83.7 us -> none  [the longest x2 16.4 us: line_backward(): jnp.einsum('nhlm,' + q_spec + '->' + k_spec, grad_scores, q_proj, preferr...]
    all_to_all x0 -> x6, blocking collectives: none -> 64 us  [exchange(): return lax.all_to_all(values, axes, split_axis=0, concat_axis=0, tiled=True)]
    reshape x19 -> x0, local copies, waits for them, and re-layouts: 32.1 us -> none  [the longest x12 16.3 us: project(): result.astype(jnp.bfloat16).reshape(in_shape[0], in_shape[1], HEADS, HEAD)]
    pallas_call x0 -> x5, Pallas kernels: none -> 29.5 us  [the longest x1 11.4 us: body(): col_both(mid_lines, grad_lines, w_col, gain_col)]
    all_to_all x8, waiting for transfers between devices: 48 us -> 74.8 us  [exchange(): return lax.all_to_all(values, axes, split_axis=0, concat_axis=0, tiled=True)]
    convert_element_type x16 -> x2, local copies, waits for them, and re-layouts: 21.3 us -> 4.95 us  [reduce_all(): mine = (both[0].astype(F32) + both[1].astype(F32)).astype(BF16)]
    all_to_all x12 -> x0, local copies, waits for them, and re-layouts: 9.04 us -> none  [the longest x5 3.75 us: from_cols(): lax.all_to_all(values, 'row', split_axis=0, concat_axis=1, tiled=True)]
  transfers between devices with their start and end apart: 9 -> 8, of which waited for: 8 -> 7; matrix products, arithmetic and copies ran while one was open for 9% -> 5% of each run, Pallas kernels for 0% -> 7%
where the time goes in v1:
time: 250 us; the launch traced here: 248 us
  waiting for transfers between devices  74.8 us (30%)
  blocking collectives  64 us (26%)
  starting transfers between devices  50 us (20%)
  Pallas kernels  29.5 us (12%)
  local copies, waits for them, and re-layouts  19.8 us (8%)
  other arithmetic  9.33 us (4%)
    all_to_all x8, waiting for transfers between devices, exchange(): return lax.all_to_all(values, axes, split_axis=0, concat_axis=0, tiled=True)  74.8 us
    all_to_all x6, blocking collectives, exchange(): return lax.all_to_all(values, axes, split_axis=0, concat_axis=0, tiled=True)  64 us
    all_to_all x8, starting transfers between devices, exchange(): return lax.all_to_all(values, axes, split_axis=0, concat_axis=0, tiled=True)  50 us
    pallas_call x1, Pallas kernels, body(): col_both(mid_lines, grad_lines, w_col, gain_col)  11.4 us
    unnamed x23, local copies, waits for them, and re-layouts  10.5 us
    pallas_call x1, Pallas kernels, body(): row_backward(grad_rows, rows_in, qkv_row, att_row, w_row, gain_row)  9.45 us
    pallas_call x1, Pallas kernels, body(): mid_send, qkv_row, att_row = row_forward(rows_in, w_row, gain_row)  5.44 us
    convert_element_type x2, other arithmetic, reduce_all(): return whole.reshape(4, D, D).astype(F32)  5.2 us
  transfers between devices with their start and end apart: 8, of which 7 were waited for; matrix products, arithmetic and copies ran while one was open for 5% of the time, Pallas kernels for 7%

profile of v1, /device:TPU:1, one launch (start us, length us, event | category | flops | bytes accessed | tf_op | source)
XLA Modules:
  0.0 248.2 jit_solution(10928319083335412814)
XLA Ops:
  0.6 0.0 copy-start.10
  0.6 9.1 %all-to-all-start = ((bf16[16,2,16,512]{3,2,1,0:T(8,128)(2,1)}), bf16[16,2,16,512]{3,2,1,0:T(8,128)(2,1)S(1)}, u32[]{:S(2)}, u32[]{:S(2)}) async-start(bf16[16,2,16,512]{3,2,1,0:T(8,128)(2,1)} %bitcast.17), calls=%async_computation | async-start | bytes 1048576 | tf_op jit(solution)/shard_map/all_to_all | solution.py:309
  9.8 0.0 copy-start
  9.8 1.0 copy-done
  10.8 0.0 copy-start.3
  10.8 1.5 tile_to_lines.1
  12.3 8.5 %all-to-all-done.x_ref = bf16[16,2,16,512]{3,2,1,0:T(8,128)(2,1)S(1)} async-done(((bf16[16,2,16,512]{3,2,1,0:T(8,128)(2,1)}), bf16[16,2,16,512]{3,2,1,0:T(8,128)(2,1)S(1)}, u32[]{:S(2)}, u32[]{:S(2)}) %all-to-all-start) | async-done | bytes 524320 | tf_op jit(solution)/shard_map/all_to_all | solution.py:309
  20.8 4.6 %all-to-all-start.2 = ((bf16[8,2,32,512]{3,2,1,0:T(8,128)(2,1)}), bf16[8,2,32,512]{3,2,1,0:T(8,128)(2,1)S(1)}, u32[]{:S(2)}, u32[]{:S(2)}) async-start(bf16[8,2,32,512]{3,2,1,0:T(8,128)(2,1)} %tile_to_lines.1), calls=%async_computation.2 | async-start | bytes 1048576 | tf_op jit(solution)/shard_map/all_to_all | solution.py:309
  25.4 0.0 copy-done.10
  25.4 0.1 broadcast_in_dim.35
  25.5 0.1 broadcast_in_dim.36.gain_ref
  25.6 0.0 copy-done.3
  25.6 5.4 %row_forward.1 = (bf16[128,16,128]{2,1,0:T(8,128)(2,1)}, bf16[3,512,512]{2,1,0:T(8,128)(2,1)S(1)}, bf16[512,512]{1,0:T(8,128)(2,1)S(1)}) custom-call(bf16[16,2,16,512]{3,2,1,0:T(8,128)(2,1)S(1)} %all-to-all-done.x_ref, bf16[4,512,512]{2,1,0:T(8,128)(2,1)S(1)} %copy-done.3, f32[1,512]{1,0:T(1,128)S(1)} %broadcast_in_dim.36.gain_ref), custom_call_target="tpu_custom_call" | custom-call | flops 1342177280 | bytes 6291456 | tf_op jit(solution)/shard_map/row_forward/pallas_call | solution.py:328
  31.0 0.0 copy-start.5
  31.0 1.1 copy-done.5
  32.2 0.0 copy-start.7
  32.2 0.8 copy-done.7
  33.0 0.3 all-to-all-done.2.c_ref
  33.3 7.2 %all-to-all-start.1 = ((bf16[128,16,128]{2,1,0:T(8,128)(2,1)}), bf16[128,16,128]{2,1,0:T(8,128)(2,1)S(1)}, u32[]{:S(2)}, u32[]{:S(2)}) async-start(bf16[128,16,128]{2,1,0:T(8,128)(2,1)} %get-tuple-element.12), calls=%async_computation.1 | async-start | bytes 1048576 | tf_op jit(solution)/shard_map/all_to_all | solution.py:309
  40.4 0.1 broadcast_in_dim.37
  40.5 0.1 broadcast_in_dim.38.gain_ref
  40.6 12.9 %all-to-all-done.1.m_ref = bf16[128,16,128]{2,1,0:T(8,128)(2,1)S(1)} async-done(((bf16[128,16,128]{2,1,0:T(8,128)(2,1)}), bf16[128,16,128]{2,1,0:T(8,128)(2,1)S(1)}, u32[]{:S(2)}, u32[]{:S(2)}) %all-to-all-start.1) | async-done | bytes 524320 | tf_op jit(solution)/shard_map/all_to_all | solution.py:309
  53.5 0.0 copy-start.2
  53.5 1.6 copy-done.2
  55.1 11.4 %col_both.1 = (bf16[8,2,32,512]{3,2,1,0:T(8,128)(2,1)}, bf16[128,16,128]{2,1,0:T(8,128)(2,1)S(1)}, bf16[4,512,512]{2,1,0:T(8,128)(2,1)S(1)}) custom-call(bf16[128,16,128]{2,1,0:T(8,128)(2,1)S(1)} %all-to-all-done.1.m_ref, bf16[8,2,32,512]{3,2,1,0:T(8,128)(2,1)S(1)} %all-to-all-done.2.c_ref, bf16[4,512,512]{2,1,0:T(8,128)(2,1)S(1)} %copy-done.2, ...), custom_call_target="tpu_custom_call" | custom-call | flops 4026531840 | bytes 6291456 | tf_op jit(solution)/shard_map/col_both/pallas_call | solution.py:330
  66.5 6.5 %all_to_all.70 = bf16[2,1024,512]{2,1,0:T(8,128)(2,1)S(1)} all-to-all(bf16[2,1024,512]{2,1,0:T(8,128)(2,1)S(1)} %bitcast.13), channel_id=1, replica_groups=mesh['y'=4,'zl'=2,'zh'=2,'x'=4,'c'=2] {'c'}, dimensions={0} | all-to-all | bytes 4194304 | tf_op jit(solution)/shard_map/all_to_all | solution.py:309
  73.0 17.1 %all_to_all.71.g_ref = bf16[128,16,128]{2,1,0:T(8,128)(2,1)} all-to-all(bf16[128,16,128]{2,1,0:T(8,128)(2,1)S(1)} %get-tuple-element.14), channel_id=1, replica_groups=mesh['y'=4,'zl'=2,'zh'=2,'x'=4,'c'=2] {'zh','x','c','y','zl'}, dimensions={0} | all-to-all | bytes 1048576 | tf_op jit(solution)/shard_map/all_to_all | solution.py:309
  90.1 3.7 %all-to-all-start.3 = ((bf16[8,2,32,512]{3,2,1,0:T(8,128)(2,1)}), bf16[8,2,32,512]{3,2,1,0:T(8,128)(2,1)S(1)}, u32[]{:S(2)}, u32[]{:S(2)}) async-start(bf16[8,2,32,512]{3,2,1,0:T(8,128)(2,1)} %get-tuple-element.13), calls=%async_computation.3 | async-start | bytes 1048576 | tf_op jit(solution)/shard_map/all_to_all | solution.py:309
  93.8 1.3 add_convert_fusion
  95.1 2.5 convert_element_type.63
  97.6 0.0 copy-start.1
  97.6 1.0 copy-done.1
  98.6 1.6 copy-done.4
  100.2 1.4 copy-done.6
  101.6 1.0 copy-done.8
  102.7 9.5 %row_backward.1 = (bf16[16,2,16,512]{3,2,1,0:T(8,128)(2,1)}, bf16[4,512,512]{2,1,0:T(8,128)(2,1)S(1)}) custom-call(bf16[128,16,128]{2,1,0:T(8,128)(2,1)S(1)} %copy-done.1, bf16[16,2,16,512]{3,2,1,0:T(8,128)(2,1)S(1)} %all-to-all-done.x_ref, bf16[3,512,512]{2,1,0:T(8,128)(2,1)S(1)} %copy-done.6, bf16[512,512]{1,0:T(8,128)(2,1)S(1)} %copy-done.8, ...), custom_call_target="tpu_custom_call" | custom-call | flops 2818572288 | bytes 8388608 | tf_op jit(solution)/shard_map/row_backward/pallas_call | solution.py:333
  112.1 0.0 all-to-all-done.3.lines_ref
  112.1 7.4 %all_to_all.72 = bf16[2,1024,512]{2,1,0:T(8,128)(2,1)} all-to-all(bf16[2,1024,512]{2,1,0:T(8,128)(2,1)S(1)} %bitcast.12), channel_id=1, replica_groups=mesh['y'=4,'zl'=2,'zh'=2,'x'=4,'c'=2] {'c'}, dimensions={0} | all-to-all | bytes 4194304 | tf_op jit(solution)/shard_map/all_to_all | solution.py:309
  119.5 7.3 %all-to-all-start.11 = ((bf16[64,64,128]{2,1,0:T(8,128)(2,1)}), bf16[64,64,128]{2,1,0:T(8,128)(2,1)}, u32[]{:S(2)}, u32[]{:S(2)}) async-start(bf16[64,64,128]{2,1,0:T(8,128)(2,1)} %convert_element_type.63), calls=%async_computation.11 | async-start | bytes 2097152 | tf_op jit(solution)/shard_map/all_to_all | solution.py:309
  126.8 0.0 copy-done.9
  126.8 1.3 add_convert_fusion.1
  128.1 2.5 convert_element_type.57
  130.5 13.7 %all-to-all-done.11 = bf16[64,64,128]{2,1,0:T(8,128)(2,1)} async-done(((bf16[64,64,128]{2,1,0:T(8,128)(2,1)}), bf16[64,64,128]{2,1,0:T(8,128)(2,1)}, u32[]{:S(2)}, u32[]{:S(2)}) %all-to-all-start.11) | async-done | bytes 1048608 | tf_op jit(solution)/shard_map/all_to_all | solution.py:309
  144.2 4.9 %all-to-all-start.7 = ((bf16[64,64,128]{2,1,0:T(8,128)(2,1)}), bf16[64,64,128]{2,1,0:T(8,128)(2,1)S(1)}, u32[]{:S(2)}, u32[]{:S(2)}) async-start(bf16[64,64,128]{2,1,0:T(8,128)(2,1)} %convert_element_type.57), calls=%async_computation.7 | async-start | bytes 2097152 | tf_op jit(solution)/shard_map/all_to_all | solution.py:309
  149.1 1.4 reduce_sum.25
  150.5 15.6 %all-to-all-done.7 = bf16[64,64,128]{2,1,0:T(8,128)(2,1)S(1)} async-done(((bf16[64,64,128]{2,1,0:T(8,128)(2,1)}), bf16[64,64,128]{2,1,0:T(8,128)(2,1)S(1)}, u32[]{:S(2)}, u32[]{:S(2)}) %all-to-all-start.7) | async-done | bytes 1048608 | tf_op jit(solution)/shard_map/all_to_all | solution.py:309
  166.1 0.2 broadcast_in_dim.42
  166.4 19.8 %all_to_all.73 = bf16[64,64,128]{2,1,0:T(8,128)(2,1)S(1)} all-to-all(bf16[64,64,128]{2,1,0:T(8,128)(2,1)S(1)} %broadcast_in_dim.42), channel_id=1, replica_groups=mesh['y'=4,'zl'=2,'zh'=2,'x'=4,'c'=2] {'y','zl','zh','x'}, dimensions={0} | all-to-all | bytes 2097152 | tf_op jit(solution)/shard_map/all_to_all | solution.py:309
  186.2 7.7 %all-to-all-start.5 = ((bf16[16,2,16,512]{3,2,1,0:T(8,128)(2,1)}), bf16[16,2,16,512]{3,2,1,0:T(8,128)(2,1)S(1)}, u32[]{:S(2)}, u32[]{:S(2)}) async-start(bf16[16,2,16,512]{3,2,1,0:T(8,128)(2,1)} %get-tuple-element.17), calls=%async_computation.5 | async-start | bytes 1048576 | tf_op jit(solution)/shard_map/all_to_all | solution.py:309
  193.9 0.2 reduce_sum.24
  194.1 0.7 broadcast_in_dim.43
  194.7 10.3 %all-to-all-done.5 = bf16[16,2,16,512]{3,2,1,0:T(8,128)(2,1)S(1)} async-done(((bf16[16,2,16,512]{3,2,1,0:T(8,128)(2,1)}), bf16[16,2,16,512]{3,2,1,0:T(8,128)(2,1)S(1)}, u32[]{:S(2)}, u32[]{:S(2)}) %all-to-all-start.5) | async-done | bytes 524320 | tf_op jit(solution)/shard_map/all_to_all | solution.py:309
  205.0 0.1 broadcast_in_dim.44
  205.1 6.5 %all_to_all.74 = bf16[2,1024,512]{2,1,0:T(8,128)(2,1)S(1)} all-to-all(bf16[2,1024,512]{2,1,0:T(8,128)(2,1)S(1)} %broadcast_in_dim.44), channel_id=1, replica_groups=mesh['y'=4,'zl'=2,'zh'=2,'x'=4,'c'=2] {'c'}, dimensions={0} | all-to-all | bytes 4194304 | tf_op jit(solution)/shard_map/all_to_all | solution.py:309
  211.6 1.2 broadcast_in_dim.39
  212.8 5.5 %all-to-all-start.8 = ((bf16[64,64,128]{2,1,0:T(8,128)(2,1)}), bf16[64,64,128]{2,1,0:T(8,128)(2,1)}, u32[]{:S(2)}, u32[]{:S(2)}) async-start(bf16[64,64,128]{2,1,0:T(8,128)(2,1)} %broadcast_in_dim.39), calls=%async_computation.8 | async-start | bytes 2097152 | tf_op jit(solution)/shard_map/all_to_all | solution.py:309
  218.3 1.7 lines_to_tile.1
  220.1 2.6 %convert.5 = f32[4,512,512]{2,1,0:T(8,128)} convert(bf16[4,512,512]{2,1,0:T(8,128)(2,1)S(1)} %bitcast.14) | non-fusion elementwise | flops 1048576 | bytes 6291456 | tf_op jit(solution)/shard_map/convert_element_type | solution.py:320
  222.7 13.6 %all-to-all-done.8 = bf16[64,64,128]{2,1,0:T(8,128)(2,1)} async-done(((bf16[64,64,128]{2,1,0:T(8,128)(2,1)}), bf16[64,64,128]{2,1,0:T(8,128)(2,1)}, u32[]{:S(2)}, u32[]{:S(2)}) %all-to-all-start.8) | async-done | bytes 1048608 | tf_op jit(solution)/shard_map/all_to_all | solution.py:309
  236.3 1.7 broadcast_in_dim.40
  238.0 0.1 broadcast_in_dim.41
  238.1 6.7 %all_to_all.75 = bf16[2,1024,512]{2,1,0:T(8,128)(2,1)S(1)} all-to-all(bf16[2,1024,512]{2,1,0:T(8,128)(2,1)S(1)} %broadcast_in_dim.41), channel_id=1, replica_groups=mesh['y'=4,'zl'=2,'zh'=2,'x'=4,'c'=2] {'c'}, dimensions={0} | all-to-all | bytes 4194304 | tf_op jit(solution)/shard_map/all_to_all | solution.py:309
  244.8 2.6 %convert.4 = f32[4,512,512]{2,1,0:T(8,128)} convert(bf16[4,512,512]{2,1,0:T(8,128)(2,1)S(1)} %bitcast.15) | non-fusion elementwise | flops 1048576 | bytes 6291456 | tf_op jit(solution)/shard_map/convert_element_type | solution.py:320
  247.4 0.8 copy.10
  (6 shorter events, 0.0 us)
Async XLA Ops:
  0.6 24.8 %copy-start.10 = (s32[2,8]{1,0:T(2,128)S(1)}, s32[2,8]{1,0:T(2,128)}, u32[]{:S(2)}) copy-start(s32[2,8]{1,0:T(2,128)} %param.9) | copy-start | bytes 196
  0.6 20.1 %all-to-all-start = ((bf16[16,2,16,512]{3,2,1,0:T(8,128)(2,1)}), bf16[16,2,16,512]{3,2,1,0:T(8,128)(2,1)S(1)}, u32[]{:S(2)}, u32[]{:S(2)}) async-start(bf16[16,2,16,512]{3,2,1,0:T(8,128)(2,1)} %bitcast.17), calls=%async_computation | async-start | bytes 1048576 | tf_op jit(solution)/shard_map/all_to_all | solution.py:309
  9.8 1.0 copy-start
  10.8 14.8 %copy-start.3 = (bf16[4,512,512]{2,1,0:T(8,128)(2,1)S(1)}, bf16[4,512,512]{2,1,0:T(8,128)(2,1)}, u32[]{:S(2)}) copy-start(bf16[4,512,512]{2,1,0:T(8,128)(2,1)} %w_ref.5) | copy-start | bytes 6291460
  20.8 12.5 %all-to-all-start.2 = ((bf16[8,2,32,512]{3,2,1,0:T(8,128)(2,1)}), bf16[8,2,32,512]{3,2,1,0:T(8,128)(2,1)S(1)}, u32[]{:S(2)}, u32[]{:S(2)}) async-start(bf16[8,2,32,512]{3,2,1,0:T(8,128)(2,1)} %tile_to_lines.1), calls=%async_computation.2 | async-start | bytes 1048576 | tf_op jit(solution)/shard_map/all_to_all | solution.py:309
  31.0 1.1 copy-start.5
  32.2 0.8 copy-start.7
  33.3 20.2 %all-to-all-start.1 = ((bf16[128,16,128]{2,1,0:T(8,128)(2,1)}), bf16[128,16,128]{2,1,0:T(8,128)(2,1)S(1)}, u32[]{:S(2)}, u32[]{:S(2)}) async-start(bf16[128,16,128]{2,1,0:T(8,128)(2,1)} %get-tuple-element.12), calls=%async_computation.1 | async-start | bytes 1048576 | tf_op jit(solution)/shard_map/all_to_all | solution.py:309
  53.5 1.6 copy-start.2
  90.1 22.0 %all-to-all-start.3 = ((bf16[8,2,32,512]{3,2,1,0:T(8,128)(2,1)}), bf16[8,2,32,512]{3,2,1,0:T(8,128)(2,1)S(1)}, u32[]{:S(2)}, u32[]{:S(2)}) async-start(bf16[8,2,32,512]{3,2,1,0:T(8,128)(2,1)} %get-tuple-element.13), calls=%async_computation.3 | async-start | bytes 1048576 | tf_op jit(solution)/shard_map/all_to_all | solution.py:309
  97.6 1.0 copy-start.1
  98.6 1.6 copy-start.4
  100.2 1.4 copy-start.6
  101.6 1.0 copy-start.8
  119.5 7.3 %copy-start.9 = (bf16[2,1024,512]{2,1,0:T(8,128)(2,1)S(1)}, bf16[2,1024,512]{2,1,0:T(8,128)(2,1)}, u32[]{:S(2)}) copy-start(bf16[2,1024,512]{2,1,0:T(8,128)(2,1)} %all_to_all.72) | copy-start | bytes 6291460
  119.5 24.7 %all-to-all-start.11 = ((bf16[64,64,128]{2,1,0:T(8,128)(2,1)}), bf16[64,64,128]{2,1,0:T(8,128)(2,1)}, u32[]{:S(2)}, u32[]{:S(2)}) async-start(bf16[64,64,128]{2,1,0:T(8,128)(2,1)} %convert_element_type.63), calls=%async_computation.11 | async-start | bytes 2097152 | tf_op jit(solution)/shard_map/all_to_all | solution.py:309
  144.2 21.9 %all-to-all-start.7 = ((bf16[64,64,128]{2,1,0:T(8,128)(2,1)}), bf16[64,64,128]{2,1,0:T(8,128)(2,1)S(1)}, u32[]{:S(2)}, u32[]{:S(2)}) async-start(bf16[64,64,128]{2,1,0:T(8,128)(2,1)} %convert_element_type.57), calls=%async_computation.7 | async-start | bytes 2097152 | tf_op jit(solution)/shard_map/all_to_all | solution.py:309
  186.2 18.8 %all-to-all-start.5 = ((bf16[16,2,16,512]{3,2,1,0:T(8,128)(2,1)}), bf16[16,2,16,512]{3,2,1,0:T(8,128)(2,1)S(1)}, u32[]{:S(2)}, u32[]{:S(2)}) async-start(bf16[16,2,16,512]{3,2,1,0:T(8,128)(2,1)} %get-tuple-element.17), calls=%async_computation.5 | async-start | bytes 1048576 | tf_op jit(solution)/shard_map/all_to_all | solution.py:309
  212.8 23.5 %all-to-all-start.8 = ((bf16[64,64,128]{2,1,0:T(8,128)(2,1)}), bf16[64,64,128]{2,1,0:T(8,128)(2,1)}, u32[]{:S(2)}, u32[]{:S(2)}) async-start(bf16[64,64,128]{2,1,0:T(8,128)(2,1)} %broadcast_in_dim.39), calls=%async_computation.8 | async-start | bytes 2097152 | tf_op jit(solution)/shard_map/all_to_all | solution.py:309
